TPU v7x, 32 devices: a whole 2x2x4 slice. The times are simulated.
32 devices in a mesh: grp: 2 (over y), blk: 4 (over z), sub: 2 (over x), pair: 2 (over core).
Axes of the slice: x: 2, y: 2, z: 4, core: 2. Of those that a mesh axis runs over, the one named last changes fastest.
Arguments:
- grad_volume: bfloat16 [16, 128, 8192], P(('grp', 'blk', 'sub'), 'pair'), parts along dimension 0, may hold values from -6 to 6
- query_feats: bfloat16 [16384, 1024], P(('grp', 'blk')), parts along dimension 0, may hold values from -6 to 6
- support_feats: bfloat16 [16, 128, 1024], P(('grp', 'blk', 'sub'), 'pair'), parts along dimension 0, may hold values from -6 to 6
- query_kernel: float32 [3, 3], replicated, may hold values from -2 to 2
- support_kernel: float32 [3, 3], replicated, may hold values from -2 to 2
Outputs:
- query_grad: float32 [16384, 1024], P(('grp', 'blk', 'sub', 'pair')), parts along dimension 0
- support_grad: float32 [16, 128, 1024], P(('grp', 'blk', 'sub'), 'pair'), parts along dimension 0
There are 2 independent parts, one for each index of `grp`. A program takes and returns all parts, laid end to end along the dimension named above; an argument that names none is the same for every part. Nothing has to cross between parts.
All inputs are finite; a program needn't handle non-finite values.
Results may differ from a plain program's by a relative error of at most 0.0029.
Values may be sent and summed in bfloat16 or wider, within the bound.
No kernel may reach another device: no remote copies, remote signals or barrier semaphores. Data moves between devices by JAX's collectives and lax.ppermute only.
A program may use at most 64 MiB of HBM per device.

v0:
```python
import math
import jax
import jax.numpy as jnp
from jax import lax
from jax.sharding import PartitionSpec as P

QW = 128
QH = 64


def extended(cells, sides, width):
    for axis, dim in sides:
        count = lax.axis_size(axis)
        ends = count - 1
        head = lax.slice_in_dim(cells, 0, width, axis=dim)
        tail = lax.slice_in_dim(cells, cells.shape[dim] - width, cells.shape[dim], axis=dim)
        cells = jnp.concatenate(
            [
                lax.ppermute(tail, axis, [(i, (i + 1) % count) for i in range(ends)]),
                cells,
                lax.ppermute(head, axis, [((i + 1) % count, i) for i in range(ends)]),
            ],
            axis=dim,
        )
    return cells


def shifted(value, axis, steps):
    count = lax.axis_size(axis)
    pairs = [(source, (source + steps) % count) for source in range(count)]
    return lax.ppermute(value, axis, pairs)


def query_pass(volume, kernel):
    planes, columns, queries = volume.shape
    grid = volume.astype(jnp.float32).reshape(planes, columns, QH, QW)
    padded = jnp.pad(grid, ((0, 0), (0, 0), (1, 1), (1, 1)))
    total = jnp.zeros_like(grid)
    for row_shift in range(3):
        for col_shift in range(3):
            total = (
                total
                + kernel[row_shift, col_shift]
                * padded[:, :, row_shift : row_shift + QH, col_shift : col_shift + QW]
            )
    return total.reshape(planes, columns, queries)


def support_pass(rimmed, kernel, planes, columns):
    total = jnp.zeros((planes, columns, rimmed.shape[2]), jnp.float32)
    for row_shift in range(3):
        for col_shift in range(3):
            total = total + kernel[row_shift, col_shift] * rimmed[
                row_shift : row_shift + planes, col_shift : col_shift + columns
            ].astype(jnp.float32)
    return total


def shards(grad_volume, query_feats, support_feats, query_kernel, support_kernel):
    planes, columns, queries = grad_volume.shape
    rimmed = extended(grad_volume, ((("blk", "sub"), 0), ("pair", 1)), 1)
    corr_grad = (
        query_pass(grad_volume, query_kernel)
        + support_pass(rimmed, support_kernel, planes, columns)
    ).astype(jnp.bfloat16)
    moved = lax.all_to_all(corr_grad, "blk", split_axis=2, concat_axis=0, tiled=True)
    cycle_size = lax.axis_size("blk")
    own_index = lax.axis_index("blk")
    tile_len = moved.shape[2]
    tiles = moved.reshape(cycle_size, planes, columns, tile_len)
    width = query_feats.shape[1]
    scale_factor = 1.0 / math.sqrt(width)

    def project(piece_index, feat_piece, acc_piece, count):
        whole_block = lax.dynamic_index_in_dim(tiles, piece_index, 0, keepdims=False)
        block = whole_block.reshape(planes * count, tile_len)
        feat_flat = feat_piece.reshape(planes * count, width)
        query_term = lax.dot_general(
            block, feat_flat, (((0,), (0,)), ((), ())), preferred_element_type=jnp.float32
        )
        acc_new = acc_piece + jnp.dot(
            block, query_feats, preferred_element_type=jnp.float32
        ).reshape(planes, count, width)
        return (query_term, acc_new)

    query_start = jnp.zeros((tile_len, width), jnp.float32)

    def turn_one(turn_index, carry):
        query_total, feat_piece, acc_piece = carry
        term_piece, acc_piece = project(
            (own_index - turn_index) % cycle_size, feat_piece, acc_piece, columns
        )
        feat_piece = shifted(feat_piece, "blk", 1)
        acc_piece = shifted(acc_piece, "blk", 1)
        return (query_total + term_piece, feat_piece, acc_piece)

    start = (query_start, support_feats, jnp.zeros((planes, columns, width), jnp.float32))
    query_total, feat_piece, support_total = lax.fori_loop(0, cycle_size, turn_one, start)
    query_grad = (
        lax.psum_scatter(query_total, ("sub", "pair"), scatter_dimension=0, tiled=True)
        * scale_factor
    )
    return (query_grad, support_total * scale_factor)


def solution(mesh):
    in_specs = (
        P(("grp", "blk", "sub"), "pair", None),
        P(("grp", "blk"), None),
        P(("grp", "blk", "sub"), "pair", None),
        P(),
        P(),
    )
    out_specs = (P(("grp", "blk", "sub", "pair"), None), P(("grp", "blk", "sub"), "pair", None))
    return jax.shard_map(shards, mesh=mesh, in_specs=in_specs, out_specs=out_specs, check_vma=False)
```

profile of v0, /device:TPU:0, one launch (start us, length us, event | category | flops | bytes accessed | tf_op | source)
XLA Modules:
  0.0 318.6 jit_solution(11927447084421412007)
XLA Ops:
  7.2 5.0 %collective-permute-start.2 = (bf16[1,64,8192]{2,1,0:T(8,128)(2,1)}, bf16[1,64,8192]{2,1,0:T(8,128)(2,1)S(1)}, u32[]{:S(2)}, u32[]{:S(2)}) collective-permute-start(bf16[1,64,8192]{2,1,0:T(8,128)(2,1)} %param.7), channel_id=1, source_target_pairs={{0,2},{2,4},{4,6},{6,8},{8,10},{10,12},{12,14},{1,3},{3,5},{5,7},{... | collective-permute-start | bytes 3145736 | tf_op jit(solution)/shard_map/ppermute | solution.py:19
  12.2 1.3 collective-permute-start.3
  13.5 1.7 fusion.33
  15.2 1.7 fusion.32
  16.9 40.4 %collective-permute-done.2 = bf16[1,64,8192]{2,1,0:T(8,128)(2,1)S(1)} collective-permute-done((bf16[1,64,8192]{2,1,0:T(8,128)(2,1)}, bf16[1,64,8192]{2,1,0:T(8,128)(2,1)S(1)}, u32[]{:S(2)}, u32[]{:S(2)}) %collective-permute-start.2) | collective-permute-done | bytes 1048608 | tf_op jit(solution)/shard_map/ppermute | solution.py:19
  58.1 1.3 collective-permute-start.5
  59.4 3.0 collective-permute-start.4
  62.8 9.4 %fusion.23 = f32[1,64,64,128]{3,2,1,0:T(8,128)S(1)} fusion(f32[1,64,64,128]{3,2,1,0:T(8,128)S(1)} %bitcast.53, f32[]{:T(128)} %bitcast.8, f32[]{:T(128)} %bitcast.7, f32[]{:T(128)} %bitcast.6, f32[]{:T(128)} %bitcast.5, f32[]{:T(128)} %bitcast.4, f32[]{:T(128)} %bitcast.3, f32[]{:T(128)} %bitcast.2, f32[]{:T(128)} %bitcast.1, f32[]{:T(128)} %bitcast), kind=kLoop, calls=%fused_computation.35 | loop fusion | flops 8912896 | bytes 4194340 | tf_op jit(solution)/shard_map/add | solution.py:42
  72.3 1.5 reshape.56
  74.0 11.4 %fusion.14 = bf16[1,64,8192]{2,1,0:T(8,128)(2,1)S(1)} fusion(f32[1,64,8192]{2,1,0:T(8,128)} %reshape.56, bf16[1,64,8192]{2,1,0:T(8,128)(2,1)} %param.7, bf16[1,64,8192]{2,1,0:T(8,128)(2,1)} %copy-done.2, bf16[1,64,8192]{2,1,0:T(8,128)(2,1)S(1)} %collective-permute-done.2, bf16[3,1,8192]{2,1,0:T(2,128)(2,1)S(1)} %copy.17, bf16[3,64,8192]{2,1,0:T(8,128)(2,1)} %copy-done, ...), kind=kLoop, calls=%fused_computation.26 | loop fusion | flops 24117248 | bytes 9535524 | tf_op jit(solution)/shard_map/convert_element_type | solution.py:65
  85.4 6.8 %copy.18 = bf16[1,64,8192]{1,0,2:T(2,128)(2,1)} copy(bf16[1,64,8192]{2,1,0:T(8,128)(2,1)S(1)} %fusion.14) | data formatting | bytes 2097152 | tf_op jit(solution)/shard_map/convert_element_type | solution.py:65
  92.7 45.2 %reduce = bf16[8192,64]{1,0:T(8,128)(2,1)S(1)} reduce(bf16[8192,1,64]{2,1,0:T(2,128)(2,1)} %bitcast.51, bf16[]{:T(256)} %broadcast.17), dimensions={1}, to_apply=%bitcast.38.reduce_sub_computation | reduce | bytes 2097154
  138.0 2.7 reshape.60
  140.6 6.3 %all-to-all-start = ((bf16[4,2,65536]{2,1,0:T(2,128)(2,1)}), bf16[4,2,65536]{2,1,0:T(2,128)(2,1)S(1)}, u32[]{:S(2)}, u32[]{:S(2)}) async-start(bf16[4,2,65536]{2,1,0:T(2,128)(2,1)} %reshape.60), calls=%async_computation | async-start | bytes 2097152 | tf_op jit(solution)/shard_map/all_to_all | solution.py:66
  146.9 25.3 %all-to-all-done = bf16[4,2,65536]{2,1,0:T(2,128)(2,1)S(1)} async-done(((bf16[4,2,65536]{2,1,0:T(2,128)(2,1)}), bf16[4,2,65536]{2,1,0:T(2,128)(2,1)S(1)}, u32[]{:S(2)}, u32[]{:S(2)}) %all-to-all-start) | async-done | bytes 1048608 | tf_op jit(solution)/shard_map/all_to_all | solution.py:66
  172.2 3.2 reshape.61
  175.4 8.2 %copy.19 = bf16[1,64,8192]{2,1,0:T(8,128)(2,1)S(1)} copy(bf16[1,64,8192]{1,0,2:T(2,128)(2,1)} %bitcast.52) | data formatting | bytes 2097152 | tf_op jit(solution)/shard_map/all_to_all | solution.py:66
  185.0 52.0 %while.20 = (s32[]{:T(128)}, f32[2048,1024]{1,0:T(8,128)}, bf16[1,64,1024]{2,1,0:T(8,128)(2,1)S(1)}, f32[1,64,1024]{2,1,0:T(8,128)S(1)}, s32[]{:T(128)}, /*index...) while((s32[]{:T(128)}, f32[2048,1024]{1,0:T(8,128)}, ...), condition=%wide.region_1.2_spmd.clone, body=%wide.region_0.1_spmd.clone.sunk | while | flops 541130752 | bytes 23986536 | solution.py:98
  185.1 3.0 fusion.44
  188.4 4.5 %select_add_fusion.2 = f32[2048,1024]{1,0:T(8,128)} fusion(f32[2048,1024]{1,0:T(8,128)} %get-tuple-element.318, pred[]{:T(512)S(6)} %compare.5, bf16[4,1,64,2048]{3,2,1,0:T(8,128)(2,1)S(1)} %get-tuple-element.333, s32[]{:T(128)S(6)} %select_n.36, bf16[1,64,1024]{2,1,0:T(8,128)(2,1)S(1)} %copy.32), kind=kOutput, calls=%fused_computation.clone.1 | convolution fusion | flops 272629760 | bytes 17170436 | tf_op jit(solution)/shard_map/while/body/eval_jaxpr/dot_general | solution.py:78
  192.9 4.6 %collective-permute-done.1 = f32[1,64,1024]{2,1,0:T(8,128)S(1)} collective-permute-done((f32[1,64,1024]{2,1,0:T(8,128)S(1)}, f32[1,64,1024]{2,1,0:T(8,128)S(1)}, u32[]{:S(2)}, u32[]{:S(2)}) %collective-permute-start.1) | collective-permute-done | bytes 262176 | tf_op jit(solution)/shard_map/while/body/eval_jaxpr/ppermute | solution.py:31
  197.5 3.0 fusion.44
  200.8 7.9 %select_add_fusion.2 = f32[2048,1024]{1,0:T(8,128)} fusion(f32[2048,1024]{1,0:T(8,128)} %get-tuple-element.318, pred[]{:T(512)S(6)} %compare.5, bf16[4,1,64,2048]{3,2,1,0:T(8,128)(2,1)S(1)} %get-tuple-element.333, s32[]{:T(128)S(6)} %select_n.36, bf16[1,64,1024]{2,1,0:T(8,128)(2,1)S(1)} %copy.32), kind=kOutput, calls=%fused_computation.clone.1 | convolution fusion | flops 272629760 | bytes 17170436 | tf_op jit(solution)/shard_map/while/body/eval_jaxpr/dot_general | solution.py:78
  209.9 1.3 collective-permute-start
  211.2 3.0 fusion.44
  214.2 2.4 collective-permute-start.1
  216.6 7.9 %select_add_fusion.2 = f32[2048,1024]{1,0:T(8,128)} fusion(f32[2048,1024]{1,0:T(8,128)} %get-tuple-element.318, pred[]{:T(512)S(6)} %compare.5, bf16[4,1,64,2048]{3,2,1,0:T(8,128)(2,1)S(1)} %get-tuple-element.333, s32[]{:T(128)S(6)} %select_n.36, bf16[1,64,1024]{2,1,0:T(8,128)(2,1)S(1)} %copy.32), kind=kOutput, calls=%fused_computation.clone.1 | convolution fusion | flops 272629760 | bytes 17170436 | tf_op jit(solution)/shard_map/while/body/eval_jaxpr/dot_general | solution.py:78
  224.6 3.0 fusion.44
  227.6 1.4 collective-permute-start.1
  229.0 7.9 %select_add_fusion.2 = f32[2048,1024]{1,0:T(8,128)} fusion(f32[2048,1024]{1,0:T(8,128)} %get-tuple-element.318, pred[]{:T(512)S(6)} %compare.5, bf16[4,1,64,2048]{3,2,1,0:T(8,128)(2,1)S(1)} %get-tuple-element.333, s32[]{:T(128)S(6)} %select_n.36, bf16[1,64,1024]{2,1,0:T(8,128)(2,1)S(1)} %copy.32), kind=kOutput, calls=%fused_computation.clone.1 | convolution fusion | flops 272629760 | bytes 17170436 | tf_op jit(solution)/shard_map/while/body/eval_jaxpr/dot_general | solution.py:78
  237.7 70.9 %reduce-scatter.2.cloned.1.call-done = f32[512,1024]{1,0:T(8,128)} async-done(((f32[2048,1024]{1,0:T(8,128)}), f32[512,1024]{1,0:T(8,128)}) %reduce-scatter.2.cloned.1.call-update) | async-done | bytes 2097168 | tf_op jit(solution)/shard_map/reduce_scatter | solution.py:100
  308.5 3.2 %broadcast_multiply_fusion = f32[512,1024]{1,0:T(8,128)} fusion(f32[512,1024]{1,0:T(8,128)} %reduce-scatter.2.cloned.1.call-done), kind=kLoop, calls=%fused_computation.45 | loop fusion | flops 524288 | bytes 4194304 | tf_op jit(solution)/shard_map/mul | solution.py:100
  (44 shorter events, 5.8 us)
Async XLA Ops:
  7.2 50.3 %copy-start.3 = (bf16[1,64,8192]{2,1,0:T(8,128)(2,1)S(1)}, bf16[1,64,8192]{2,1,0:T(8,128)(2,1)}, u32[]{:S(2)}) copy-start(bf16[1,64,8192]{2,1,0:T(8,128)(2,1)} %param.7) | copy-start | bytes 3145732
  7.2 50.2 %collective-permute-start.2 = (bf16[1,64,8192]{2,1,0:T(8,128)(2,1)}, bf16[1,64,8192]{2,1,0:T(8,128)(2,1)S(1)}, u32[]{:S(2)}, u32[]{:S(2)}) collective-permute-start(bf16[1,64,8192]{2,1,0:T(8,128)(2,1)} %param.7), channel_id=1, source_target_pairs={{0,2},{2,4},{4,6},{6,8},{8,10},{10,12},{12,14},{1,3},{3,5},{5,7},{... | collective-permute-start | bytes 3145736 | tf_op jit(solution)/shard_map/ppermute | solution.py:19
  12.2 45.5 %collective-permute-start.3 = (bf16[1,64,8192]{2,1,0:T(8,128)(2,1)}, bf16[1,64,8192]{2,1,0:T(8,128)(2,1)S(1)}, u32[]{:S(2)}, u32[]{:S(2)}) collective-permute-start(bf16[1,64,8192]{2,1,0:T(8,128)(2,1)} %param.7), channel_id=1, source_target_pairs={{2,0},{4,2},{6,4},{8,6},{10,8},{12,10},{14,12},{3,1},{5,3},{7,5},{... | collective-permute-start | bytes 3145736 | tf_op jit(solution)/shard_map/ppermute | solution.py:21
  57.7 5.1 %copy-start.2 = (bf16[1,64,8192]{2,1,0:T(8,128)(2,1)}, bf16[1,64,8192]{2,1,0:T(8,128)(2,1)S(1)}, u32[]{:S(2)}) copy-start(bf16[1,64,8192]{2,1,0:T(8,128)(2,1)S(1)} %collective-permute-done.3) | copy-start | bytes 3145732
  57.8 5.1 %copy-start = (bf16[3,64,8192]{2,1,0:T(8,128)(2,1)}, bf16[3,64,8192]{2,1,0:T(8,128)(2,1)S(1)}, u32[]{:S(2)}) copy-start(bf16[3,64,8192]{2,1,0:T(8,128)(2,1)S(1)} %constant_dynamic-update-slice_fusion) | copy-start | bytes 9437188
  58.1 15.7 %collective-permute-start.5 = (bf16[3,1,8192]{2,0,1:T(4,128)(2,1)S(1)}, bf16[3,1,8192]{2,0,1:T(4,128)(2,1)S(1)}, u32[]{:S(2)}, u32[]{:S(2)}) collective-permute-start(bf16[3,1,8192]{2,0,1:T(4,128)(2,1)S(1)} %copy.22), channel_id=1, source_target_pairs={{1,0},{3,2},{5,4},{7,6},{9,8},{11,10},{13,12},{15,14},{17,16},{19,... | collective-permute-start | bytes 147464 | tf_op jit(solution)/shard_map/ppermute | solution.py:21
  59.4 14.5 %collective-permute-start.4 = (bf16[3,1,8192]{2,0,1:T(4,128)(2,1)S(1)}, bf16[3,1,8192]{2,0,1:T(4,128)(2,1)S(1)}, u32[]{:S(2)}, u32[]{:S(2)}) collective-permute-start(bf16[3,1,8192]{2,0,1:T(4,128)(2,1)S(1)} %copy.21), channel_id=1, source_target_pairs={{0,1},{2,3},{4,5},{6,7},{8,9},{10,11},{12,13},{14,15},{16,17},{18,... | collective-permute-start | bytes 147464 | tf_op jit(solution)/shard_map/ppermute | solution.py:19
  140.6 31.6 %all-to-all-start = ((bf16[4,2,65536]{2,1,0:T(2,128)(2,1)}), bf16[4,2,65536]{2,1,0:T(2,128)(2,1)S(1)}, u32[]{:S(2)}, u32[]{:S(2)}) async-start(bf16[4,2,65536]{2,1,0:T(2,128)(2,1)} %reshape.60), calls=%async_computation | async-start | bytes 2097152 | tf_op jit(solution)/shard_map/all_to_all | solution.py:66
  146.9 161.6 %reduce-scatter.2.cloned.1.call-start = ((), (), s32[]{:S(2)}) async-start(), calls=%async_computation.2 | async-start | bytes 10485760 | tf_op jit(solution)/shard_map/reduce_scatter | solution.py:100
  183.5 1.4 copy-start.1
  185.0 7.9 %collective-permute-start = (bf16[1,64,1024]{2,1,0:T(8,128)(2,1)S(1)}, bf16[1,64,1024]{2,1,0:T(8,128)(2,1)S(1)}, u32[]{:S(2)}, u32[]{:S(2)}) collective-permute-start(bf16[1,64,1024]{2,1,0:T(8,128)(2,1)S(1)} %copy.32), channel_id=1, source_target_pairs={{0,4},{4,8},{8,12},{12,0},{1,5},{5,9},{9,13},{13,1},{2,6},{6,10},{... | collective-permute-start | bytes 393224 | tf_op jit(solution)/shard_map/while/body/eval_jaxpr/ppermute | solution.py:31
  188.1 9.3 %collective-permute-start.1 = (f32[1,64,1024]{2,1,0:T(8,128)S(1)}, f32[1,64,1024]{2,1,0:T(8,128)S(1)}, u32[]{:S(2)}, u32[]{:S(2)}) collective-permute-start(f32[1,64,1024]{2,1,0:T(8,128)S(1)} %fusion.44), channel_id=1, source_target_pairs={{0,4},{4,8},{8,12},{12,0},{1,5},{5,9},{9,13},{13,1},{2,6},{6,10},{... | collective-permute-start | bytes 786440 | tf_op jit(solution)/shard_map/while/body/eval_jaxpr/ppermute | solution.py:31
  197.4 11.2 %collective-permute-start = (bf16[1,64,1024]{2,1,0:T(8,128)(2,1)S(1)}, bf16[1,64,1024]{2,1,0:T(8,128)(2,1)S(1)}, u32[]{:S(2)}, u32[]{:S(2)}) collective-permute-start(bf16[1,64,1024]{2,1,0:T(8,128)(2,1)S(1)} %copy.32), channel_id=1, source_target_pairs={{0,4},{4,8},{8,12},{12,0},{1,5},{5,9},{9,13},{13,1},{2,6},{6,10},{... | collective-permute-start | bytes 393224 | tf_op jit(solution)/shard_map/while/body/eval_jaxpr/ppermute | solution.py:31
  200.6 9.3 %collective-permute-start.1 = (f32[1,64,1024]{2,1,0:T(8,128)S(1)}, f32[1,64,1024]{2,1,0:T(8,128)S(1)}, u32[]{:S(2)}, u32[]{:S(2)}) collective-permute-start(f32[1,64,1024]{2,1,0:T(8,128)S(1)} %fusion.44), channel_id=1, source_target_pairs={{0,4},{4,8},{8,12},{12,0},{1,5},{5,9},{9,13},{13,1},{2,6},{6,10},{... | collective-permute-start | bytes 786440 | tf_op jit(solution)/shard_map/while/body/eval_jaxpr/ppermute | solution.py:31
  209.9 14.6 %collective-permute-start = (bf16[1,64,1024]{2,1,0:T(8,128)(2,1)S(1)}, bf16[1,64,1024]{2,1,0:T(8,128)(2,1)S(1)}, u32[]{:S(2)}, u32[]{:S(2)}) collective-permute-start(bf16[1,64,1024]{2,1,0:T(8,128)(2,1)S(1)} %copy.32), channel_id=1, source_target_pairs={{0,4},{4,8},{8,12},{12,0},{1,5},{5,9},{9,13},{13,1},{2,6},{6,10},{... | collective-permute-start | bytes 393224 | tf_op jit(solution)/shard_map/while/body/eval_jaxpr/ppermute | solution.py:31
  214.2 10.3 %collective-permute-start.1 = (f32[1,64,1024]{2,1,0:T(8,128)S(1)}, f32[1,64,1024]{2,1,0:T(8,128)S(1)}, u32[]{:S(2)}, u32[]{:S(2)}) collective-permute-start(f32[1,64,1024]{2,1,0:T(8,128)S(1)} %fusion.44), channel_id=1, source_target_pairs={{0,4},{4,8},{8,12},{12,0},{1,5},{5,9},{9,13},{13,1},{2,6},{6,10},{... | collective-permute-start | bytes 786440 | tf_op jit(solution)/shard_map/while/body/eval_jaxpr/ppermute | solution.py:31
  224.5 12.4 %collective-permute-start = (bf16[1,64,1024]{2,1,0:T(8,128)(2,1)S(1)}, bf16[1,64,1024]{2,1,0:T(8,128)(2,1)S(1)}, u32[]{:S(2)}, u32[]{:S(2)}) collective-permute-start(bf16[1,64,1024]{2,1,0:T(8,128)(2,1)S(1)} %copy.32), channel_id=1, source_target_pairs={{0,4},{4,8},{8,12},{12,0},{1,5},{5,9},{9,13},{13,1},{2,6},{6,10},{... | collective-permute-start | bytes 393224 | tf_op jit(solution)/shard_map/while/body/eval_jaxpr/ppermute | solution.py:31
  227.6 9.3 %collective-permute-start.1 = (f32[1,64,1024]{2,1,0:T(8,128)S(1)}, f32[1,64,1024]{2,1,0:T(8,128)S(1)}, u32[]{:S(2)}, u32[]{:S(2)}) collective-permute-start(f32[1,64,1024]{2,1,0:T(8,128)S(1)} %fusion.44), channel_id=1, source_target_pairs={{0,4},{4,8},{8,12},{12,0},{1,5},{5,9},{9,13},{13,1},{2,6},{6,10},{... | collective-permute-start | bytes 786440 | tf_op jit(solution)/shard_map/while/body/eval_jaxpr/ppermute | solution.py:31
Sparse Core Ops, SparseCore 0:
  237.1 71.4 reduce-scatter.1
where the time goes:
time: 320 us; the launch traced here: 319 us
  waiting for transfers between devices  142 us (44%)
  other arithmetic  70.3 us (22%)
  matrix products  40.3 us (13%)
  local copies, waits for them, and re-layouts  28.6 us (9%)
  starting transfers between devices  22.6 us (7%)
  between operations  14.2 us (4%)
    reduce_scatter x1, waiting for transfers between devices, shards(): lax.psum_scatter(query_total, ('sub', 'pair'), scatter_dimension=0, tiled...  70.9 us
    unnamed x3, other arithmetic  45.5 us
    ppermute x2, waiting for transfers between devices, extended(): lax.ppermute(tail, axis, [(i, (i + 1) % count) for i in range(ends)])  40.4 us
    dot_general x4, matrix products, project(): lax.dot_general(block, feat_flat, (((0,), (0,)), ((), ())), preferred_ele...  28.1 us
    all_to_all x1, waiting for transfers between devices, shards(): lax.all_to_all(corr_grad, 'blk', split_axis=2, concat_axis=0, tiled=True)  25.3 us
    dot_general x4, matrix products, project(): jnp.dot(block, query_feats, preferred_element_type=jnp.float32)  12.1 us
    convert_element_type x1, other arithmetic, shards(): corr_grad = (query_pass(grad_volume, query_kernel) + support_pass(rimmed,...  11.4 us
    add x1, other arithmetic, query_pass(): total + kernel[row_shift, col_shift] * padded[:, :, row_shift:row_shift +...  9.43 us
  transfers between devices with their start and end apart: 14, of which 5 were waited for; matrix products, arithmetic and copies ran while one was open for 18% of the time, Pallas kernels for 0%

commit v1 on v0

--- a/solution.py
+++ b/solution.py
@@ -6,6 +6,18 @@
 
 QW = 128
 QH = 64
+
+
+def rotated_exchange(x, axis, split, join):
+    ways, here = (lax.axis_size(axis), lax.axis_index(axis))
+    width = x.shape[split] // ways
+    turned = jnp.roll(x, -here * width, axis=split)
+    got = [lax.slice_in_dim(turned, 0, width, axis=split)]
+    for far in range(1, ways):
+        sent = lax.slice_in_dim(turned, far * width, (far + 1) * width, axis=split)
+        got.append(lax.ppermute(sent, axis, [(d, (d + far) % ways) for d in range(ways)]))
+    line = jnp.concatenate(got[::-1], axis=join)
+    return jnp.roll(line, (here + 1) * got[0].shape[join], axis=join)
 
 
 def extended(cells, sides, width):
@@ -63,7 +75,7 @@
         query_pass(grad_volume, query_kernel)
         + support_pass(rimmed, support_kernel, planes, columns)
     ).astype(jnp.bfloat16)
-    moved = lax.all_to_all(corr_grad, "blk", split_axis=2, concat_axis=0, tiled=True)
+    moved = rotated_exchange(corr_grad, "blk", 2, 0)
     cycle_size = lax.axis_size("blk")
     own_index = lax.axis_index("blk")
     tile_len = moved.shape[2]

time: 320 us -> 250 us (0.78)
  other arithmetic: 70.3 us -> 25.5 us
  local copies, waits for them, and re-layouts: 28.6 us -> 6.63 us
  waiting for transfers between devices: 142 us -> 137 us
    unnamed x3 -> x2, other arithmetic: 45.5 us -> 0.24 us
    all_to_all x1 -> x0, waiting for transfers between devices: 25.3 us -> none  [shards(): lax.all_to_all(corr_grad, 'blk', split_axis=2, concat_axis=0, tiled=True)]
    ppermute x0 -> x3, waiting for transfers between devices: none -> 22.3 us  [rotated_exchange(): lax.ppermute(sent, axis, [(d, (d + far) % ways) for d in range(ways)])]
    all_to_all x2 -> x0, local copies, waits for them, and re-layouts: 8.96 us -> none  [shards(): lax.all_to_all(corr_grad, 'blk', split_axis=2, concat_axis=0, tiled=True)]
    convert_element_type x1 -> x0, local copies, waits for them, and re-layouts: 6.78 us -> none  [shards(): corr_grad = (query_pass(grad_volume, query_kernel) + support_pass(rimmed,...]
    ppermute x0 -> x3, starting transfers between devices: none -> 6.72 us  [rotated_exchange(): lax.ppermute(sent, axis, [(d, (d + far) % ways) for d in range(ways)])]
    all_to_all x1 -> x0, starting transfers between devices: 6.3 us -> none  [shards(): lax.all_to_all(corr_grad, 'blk', split_axis=2, concat_axis=0, tiled=True)]
    unnamed x16 -> x17, local copies, waits for them, and re-layouts: 7.52 us -> 1.27 us
  transfers between devices with their start and end apart: 14 -> 16, of which waited for: 5 -> 6; matrix products, arithmetic and copies ran while one was open for 18% -> 23% of each run, Pallas kernels for 0% -> 0%
where the time goes in v1:
time: 250 us; the launch traced here: 249 us
  waiting for transfers between devices  137 us (55%)
  matrix products  40.3 us (16%)
  starting transfers between devices  25.7 us (10%)
  other arithmetic  25.5 us (10%)
  between operations  14.3 us (6%)
  local copies, waits for them, and re-layouts  6.63 us (3%)
    reduce_scatter x1, waiting for transfers between devices, shards(): lax.psum_scatter(query_total, ('sub', 'pair'), scatter_dimension=0, tiled...  71 us
    ppermute x2, waiting for transfers between devices, extended(): lax.ppermute(tail, axis, [(i, (i + 1) % count) for i in range(ends)])  40.4 us
    dot_general x4, matrix products, project(): lax.dot_general(block, feat_flat, (((0,), (0,)), ((), ())), preferred_ele...  28.2 us
    ppermute x3, waiting for transfers between devices, rotated_exchange(): lax.ppermute(sent, axis, [(d, (d + far) % ways) for d in range(ways)])  22.3 us
    dot_general x4, matrix products, project(): jnp.dot(block, query_feats, preferred_element_type=jnp.float32)  12.1 us
    convert_element_type x1, other arithmetic, shards(): corr_grad = (query_pass(grad_volume, query_kernel) + support_pass(rimmed,...  11.2 us
    ppermute x8, starting transfers between devices, shifted(): return lax.ppermute(value, axis, pairs)  10 us
    add x1, other arithmetic, query_pass(): total + kernel[row_shift, col_shift] * padded[:, :, row_shift:row_shift +...  9.59 us
  transfers between devices with their start and end apart: 16, of which 6 were waited for; matrix products, arithmetic and copies ran while one was open for 23% of the time, Pallas kernels for 0%

profile of v1, /device:TPU:0, one launch (start us, length us, event | category | flops | bytes accessed | tf_op | source)
XLA Modules:
  0.0 249.3 jit_solution(10874276899575807985)
XLA Ops:
  7.2 5.0 %collective-permute-start.2 = (bf16[1,64,8192]{2,1,0:T(8,128)(2,1)}, bf16[1,64,8192]{2,1,0:T(8,128)(2,1)S(1)}, u32[]{:S(2)}, u32[]{:S(2)}) collective-permute-start(bf16[1,64,8192]{2,1,0:T(8,128)(2,1)} %param.7), channel_id=1, source_target_pairs={{0,2},{2,4},{4,6},{6,8},{8,10},{10,12},{12,14},{1,3},{3,5},{5,7},{... | collective-permute-start | bytes 3145736 | tf_op jit(solution)/shard_map/ppermute | solution.py:31
  12.3 1.3 collective-permute-start.3
  13.6 1.7 fusion.35
  15.3 1.7 fusion.34
  17.0 40.4 %collective-permute-done.2 = bf16[1,64,8192]{2,1,0:T(8,128)(2,1)S(1)} collective-permute-done((bf16[1,64,8192]{2,1,0:T(8,128)(2,1)}, bf16[1,64,8192]{2,1,0:T(8,128)(2,1)S(1)}, u32[]{:S(2)}, u32[]{:S(2)}) %collective-permute-start.2) | collective-permute-done | bytes 1048608 | tf_op jit(solution)/shard_map/ppermute | solution.py:31
  58.0 1.3 collective-permute-start.4
  59.3 1.3 collective-permute-start.5
  61.0 9.6 %fusion.23 = f32[1,64,64,128]{3,2,1,0:T(8,128)S(1)} fusion(f32[1,64,64,128]{3,2,1,0:T(8,128)S(1)} %bitcast.50, f32[]{:T(128)} %bitcast.8, f32[]{:T(128)} %bitcast.7, f32[]{:T(128)} %bitcast.6, f32[]{:T(128)} %bitcast.5, f32[]{:T(128)} %bitcast.4, f32[]{:T(128)} %bitcast.3, f32[]{:T(128)} %bitcast.2, f32[]{:T(128)} %bitcast.1, f32[]{:T(128)} %bitcast), kind=kLoop, calls=%fused_computation.35 | loop fusion | flops 8912896 | bytes 4194340 | tf_op jit(solution)/shard_map/add | solution.py:54
  70.6 1.5 reshape.57
  72.1 11.2 %fusion.14 = bf16[1,64,8192]{2,1,0:T(8,128)(2,1)S(1)} fusion(f32[1,64,8192]{2,1,0:T(8,128)} %reshape.57, bf16[1,64,8192]{2,1,0:T(8,128)(2,1)} %param.7, bf16[1,64,8192]{2,1,0:T(8,128)(2,1)} %copy-done.2, bf16[1,64,8192]{2,1,0:T(8,128)(2,1)S(1)} %collective-permute-done.2, bf16[3,1,8192]{2,1,0:T(2,128)(2,1)S(1)} %collective-permute-done.5, ...), kind=kLoop, calls=%fused_computation.26 | loop fusion | flops 24117248 | bytes 9535524 | tf_op jit(solution)/shard_map/convert_element_type | solution.py:77
  83.9 5.7 %collective-permute-start.6 = (bf16[1,64,2048]{2,1,0:T(8,128)(2,1)S(1)}, bf16[1,64,2048]{2,1,0:T(8,128)(2,1)S(1)}, u32[]{:S(2)}, u32[]{:S(2)}) collective-permute-start(bf16[1,64,2048]{2,1,0:T(8,128)(2,1)S(1)} %get-tuple-element.224), channel_id=1, source_target_pairs={{0,12},{4,0},{8,4},{12,8},{1,13},{5,1},{9,5},{13,9},{2,14},{6,2},{... | collective-permute-start | bytes 786440 | tf_op jit(solution)/shard_map/ppermute | solution.py:18
  89.7 1.0 collective-permute-start.8
  90.7 5.6 %collective-permute-done.6 = bf16[1,64,2048]{2,1,0:T(8,128)(2,1)S(1)} collective-permute-done((bf16[1,64,2048]{2,1,0:T(8,128)(2,1)S(1)}, bf16[1,64,2048]{2,1,0:T(8,128)(2,1)S(1)}, u32[]{:S(2)}, u32[]{:S(2)}) %collective-permute-start.6) | collective-permute-done | bytes 262176 | tf_op jit(solution)/shard_map/ppermute | solution.py:18
  96.3 16.6 %collective-permute-done.7 = bf16[1,64,2048]{2,1,0:T(8,128)(2,1)S(1)} collective-permute-done((bf16[1,64,2048]{2,1,0:T(8,128)(2,1)S(1)}, bf16[1,64,2048]{2,1,0:T(8,128)(2,1)S(1)}, u32[]{:S(2)}, u32[]{:S(2)}) %collective-permute-start.7) | collective-permute-done | bytes 262176 | tf_op jit(solution)/shard_map/ppermute | solution.py:18
  114.0 53.6 %while.20 = (s32[]{:T(128)}, f32[2048,1024]{1,0:T(8,128)}, bf16[1,64,1024]{2,1,0:T(8,128)(2,1)S(1)}, f32[1,64,1024]{2,1,0:T(8,128)S(1)}, s32[]{:T(128)}, /*index...) while((s32[]{:T(128)}, f32[2048,1024]{1,0:T(8,128)}, ...), condition=%wide.region_1.2_spmd.clone, body=%wide.region_0.1_spmd.clone.sunk | while | flops 541130752 | bytes 23986536 | solution.py:110
  114.0 1.2 collective-permute-start
  115.2 3.0 %fusion.46 = f32[1,64,1024]{2,1,0:T(8,128)S(1)} fusion(f32[1,64,1024]{2,1,0:T(8,128)S(1)} %get-tuple-element.302, bf16[2048,1024]{1,0:T(8,128)(2,1)} %get-tuple-element.316, bf16[4,1,64,2048]{3,2,1,0:T(8,128)(2,1)S(1)} %get-tuple-element.315, s32[]{:T(128)S(6)} %select_n.62), kind=kOutput, calls=%fused_computation.2.clone.1 | convolution fusion | flops 268500992 | bytes 4980740 | tf_op jit(solution)/shard_map/while/body/eval_jaxpr/dot_general | solution.py:93
  118.2 2.5 %collective-permute-start.1 = (f32[1,64,1024]{2,1,0:T(8,128)S(1)}, f32[1,64,1024]{2,1,0:T(8,128)S(1)}, u32[]{:S(2)}, u32[]{:S(2)}) collective-permute-start(f32[1,64,1024]{2,1,0:T(8,128)S(1)} %fusion.46), channel_id=1, source_target_pairs={{0,4},{4,8},{8,12},{12,0},{1,5},{5,9},{9,13},{13,1},{2,6},{6,10},{... | collective-permute-start | bytes 786440 | tf_op jit(solution)/shard_map/while/body/eval_jaxpr/ppermute | solution.py:43
  120.8 4.5 %select_add_fusion.2 = f32[2048,1024]{1,0:T(8,128)} fusion(f32[2048,1024]{1,0:T(8,128)} %get-tuple-element.300, pred[]{:T(512)S(6)} %compare.7, bf16[4,1,64,2048]{3,2,1,0:T(8,128)(2,1)S(1)} %get-tuple-element.315, s32[]{:T(128)S(6)} %select_n.62, bf16[1,64,1024]{2,1,0:T(8,128)(2,1)S(1)} %copy.23), kind=kOutput, calls=%fused_computation.clone.1 | convolution fusion | flops 272629760 | bytes 17170436 | tf_op jit(solution)/shard_map/while/body/eval_jaxpr/dot_general | solution.py:90
  125.3 2.7 %collective-permute-done.1 = f32[1,64,1024]{2,1,0:T(8,128)S(1)} collective-permute-done((f32[1,64,1024]{2,1,0:T(8,128)S(1)}, f32[1,64,1024]{2,1,0:T(8,128)S(1)}, u32[]{:S(2)}, u32[]{:S(2)}) %collective-permute-start.1) | collective-permute-done | bytes 262176 | tf_op jit(solution)/shard_map/while/body/eval_jaxpr/ppermute | solution.py:43
  128.7 3.0 %fusion.46 = f32[1,64,1024]{2,1,0:T(8,128)S(1)} fusion(f32[1,64,1024]{2,1,0:T(8,128)S(1)} %get-tuple-element.302, bf16[2048,1024]{1,0:T(8,128)(2,1)} %get-tuple-element.316, bf16[4,1,64,2048]{3,2,1,0:T(8,128)(2,1)S(1)} %get-tuple-element.315, s32[]{:T(128)S(6)} %select_n.62), kind=kOutput, calls=%fused_computation.2.clone.1 | convolution fusion | flops 268500992 | bytes 4980740 | tf_op jit(solution)/shard_map/while/body/eval_jaxpr/dot_general | solution.py:93
  132.2 7.9 %select_add_fusion.2 = f32[2048,1024]{1,0:T(8,128)} fusion(f32[2048,1024]{1,0:T(8,128)} %get-tuple-element.300, pred[]{:T(512)S(6)} %compare.7, bf16[4,1,64,2048]{3,2,1,0:T(8,128)(2,1)S(1)} %get-tuple-element.315, s32[]{:T(128)S(6)} %select_n.62, bf16[1,64,1024]{2,1,0:T(8,128)(2,1)S(1)} %copy.23), kind=kOutput, calls=%fused_computation.clone.1 | convolution fusion | flops 272629760 | bytes 17170436 | tf_op jit(solution)/shard_map/while/body/eval_jaxpr/dot_general | solution.py:90
  140.5 0.8 collective-permute-start
  141.2 3.0 %fusion.46 = f32[1,64,1024]{2,1,0:T(8,128)S(1)} fusion(f32[1,64,1024]{2,1,0:T(8,128)S(1)} %get-tuple-element.302, bf16[2048,1024]{1,0:T(8,128)(2,1)} %get-tuple-element.316, bf16[4,1,64,2048]{3,2,1,0:T(8,128)(2,1)S(1)} %get-tuple-element.315, s32[]{:T(128)S(6)} %select_n.62), kind=kOutput, calls=%fused_computation.2.clone.1 | convolution fusion | flops 268500992 | bytes 4980740 | tf_op jit(solution)/shard_map/while/body/eval_jaxpr/dot_general | solution.py:93
  144.3 2.9 %collective-permute-start.1 = (f32[1,64,1024]{2,1,0:T(8,128)S(1)}, f32[1,64,1024]{2,1,0:T(8,128)S(1)}, u32[]{:S(2)}, u32[]{:S(2)}) collective-permute-start(f32[1,64,1024]{2,1,0:T(8,128)S(1)} %fusion.46), channel_id=1, source_target_pairs={{0,4},{4,8},{8,12},{12,0},{1,5},{5,9},{9,13},{13,1},{2,6},{6,10},{... | collective-permute-start | bytes 786440 | tf_op jit(solution)/shard_map/while/body/eval_jaxpr/ppermute | solution.py:43
  147.2 7.9 %select_add_fusion.2 = f32[2048,1024]{1,0:T(8,128)} fusion(f32[2048,1024]{1,0:T(8,128)} %get-tuple-element.300, pred[]{:T(512)S(6)} %compare.7, bf16[4,1,64,2048]{3,2,1,0:T(8,128)(2,1)S(1)} %get-tuple-element.315, s32[]{:T(128)S(6)} %select_n.62, bf16[1,64,1024]{2,1,0:T(8,128)(2,1)S(1)} %copy.23), kind=kOutput, calls=%fused_computation.clone.1 | convolution fusion | flops 272629760 | bytes 17170436 | tf_op jit(solution)/shard_map/while/body/eval_jaxpr/dot_general | solution.py:90
  155.1 0.7 collective-permute-start
  155.8 3.0 %fusion.46 = f32[1,64,1024]{2,1,0:T(8,128)S(1)} fusion(f32[1,64,1024]{2,1,0:T(8,128)S(1)} %get-tuple-element.302, bf16[2048,1024]{1,0:T(8,128)(2,1)} %get-tuple-element.316, bf16[4,1,64,2048]{3,2,1,0:T(8,128)(2,1)S(1)} %get-tuple-element.315, s32[]{:T(128)S(6)} %select_n.62), kind=kOutput, calls=%fused_computation.2.clone.1 | convolution fusion | flops 268500992 | bytes 4980740 | tf_op jit(solution)/shard_map/while/body/eval_jaxpr/dot_general | solution.py:93
  158.9 0.8 collective-permute-start.1
  159.6 7.9 %select_add_fusion.2 = f32[2048,1024]{1,0:T(8,128)} fusion(f32[2048,1024]{1,0:T(8,128)} %get-tuple-element.300, pred[]{:T(512)S(6)} %compare.7, bf16[4,1,64,2048]{3,2,1,0:T(8,128)(2,1)S(1)} %get-tuple-element.315, s32[]{:T(128)S(6)} %select_n.62, bf16[1,64,1024]{2,1,0:T(8,128)(2,1)S(1)} %copy.23), kind=kOutput, calls=%fused_computation.clone.1 | convolution fusion | flops 272629760 | bytes 17170436 | tf_op jit(solution)/shard_map/while/body/eval_jaxpr/dot_general | solution.py:90
  168.3 71.0 %reduce-scatter.2.cloned.1.call-done = f32[512,1024]{1,0:T(8,128)} async-done(((f32[2048,1024]{1,0:T(8,128)}), f32[512,1024]{1,0:T(8,128)}) %reduce-scatter.2.cloned.1.call-update) | async-done | bytes 2097168 | tf_op jit(solution)/shard_map/reduce_scatter | solution.py:112
  239.3 3.2 %broadcast_multiply_fusion = f32[512,1024]{1,0:T(8,128)} fusion(f32[512,1024]{1,0:T(8,128)} %reduce-scatter.2.cloned.1.call-done), kind=kLoop, calls=%fused_computation.48 | loop fusion | flops 524288 | bytes 4194304 | tf_op jit(solution)/shard_map/mul | solution.py:112
  (47 shorter events, 4.9 us)
Async XLA Ops:
  7.2 50.3 %copy-start.3 = (bf16[1,64,8192]{2,1,0:T(8,128)(2,1)S(1)}, bf16[1,64,8192]{2,1,0:T(8,128)(2,1)}, u32[]{:S(2)}) copy-start(bf16[1,64,8192]{2,1,0:T(8,128)(2,1)} %param.7) | copy-start | bytes 3145732
  7.2 232.1 %reduce-scatter.2.cloned.1.call-start = ((), (), s32[]{:S(2)}) async-start(), calls=%async_computation.1 | async-start | bytes 10485760 | tf_op jit(solution)/shard_map/reduce_scatter | solution.py:112
  7.2 50.2 %collective-permute-start.2 = (bf16[1,64,8192]{2,1,0:T(8,128)(2,1)}, bf16[1,64,8192]{2,1,0:T(8,128)(2,1)S(1)}, u32[]{:S(2)}, u32[]{:S(2)}) collective-permute-start(bf16[1,64,8192]{2,1,0:T(8,128)(2,1)} %param.7), channel_id=1, source_target_pairs={{0,2},{2,4},{4,6},{6,8},{8,10},{10,12},{12,14},{1,3},{3,5},{5,7},{... | collective-permute-start | bytes 3145736 | tf_op jit(solution)/shard_map/ppermute | solution.py:31
  12.3 45.5 %collective-permute-start.3 = (bf16[1,64,8192]{2,1,0:T(8,128)(2,1)}, bf16[1,64,8192]{2,1,0:T(8,128)(2,1)S(1)}, u32[]{:S(2)}, u32[]{:S(2)}) collective-permute-start(bf16[1,64,8192]{2,1,0:T(8,128)(2,1)} %param.7), channel_id=1, source_target_pairs={{2,0},{4,2},{6,4},{8,6},{10,8},{12,10},{14,12},{3,1},{5,3},{7,5},{... | collective-permute-start | bytes 3145736 | tf_op jit(solution)/shard_map/ppermute | solution.py:33
  57.7 3.2 %copy-start.2 = (bf16[1,64,8192]{2,1,0:T(8,128)(2,1)}, bf16[1,64,8192]{2,1,0:T(8,128)(2,1)S(1)}, u32[]{:S(2)}) copy-start(bf16[1,64,8192]{2,1,0:T(8,128)(2,1)S(1)} %collective-permute-done.3) | copy-start | bytes 3145732
  57.8 3.2 %copy-start = (bf16[3,64,8192]{2,1,0:T(8,128)(2,1)}, bf16[3,64,8192]{2,1,0:T(8,128)(2,1)S(1)}, u32[]{:S(2)}) copy-start(bf16[3,64,8192]{2,1,0:T(8,128)(2,1)S(1)} %constant_dynamic-update-slice_fusion) | copy-start | bytes 9437188
  58.0 14.1 %collective-permute-start.4 = (bf16[3,1,8192]{2,1,0:T(2,128)(2,1)S(1)}, bf16[3,1,8192]{2,1,0:T(2,128)(2,1)S(1)}, u32[]{:S(2)}, u32[]{:S(2)}) collective-permute-start(bf16[3,1,8192]{2,1,0:T(2,128)(2,1)S(1)} %get-tuple-element.220), channel_id=1, source_target_pairs={{0,1},{2,3},{4,5},{6,7},{8,9},{10,11},{12,13},{14,15},{16,17},{18,... | collective-permute-start | bytes 147464 | tf_op jit(solution)/shard_map/ppermute | solution.py:31
  59.3 12.8 %collective-permute-start.5 = (bf16[3,1,8192]{2,1,0:T(2,128)(2,1)S(1)}, bf16[3,1,8192]{2,1,0:T(2,128)(2,1)S(1)}, u32[]{:S(2)}, u32[]{:S(2)}) collective-permute-start(bf16[3,1,8192]{2,1,0:T(2,128)(2,1)S(1)} %get-tuple-element.221), channel_id=1, source_target_pairs={{1,0},{3,2},{5,4},{7,6},{9,8},{11,10},{13,12},{15,14},{17,16},{19,... | collective-permute-start | bytes 147464 | tf_op jit(solution)/shard_map/ppermute | solution.py:33
  83.9 12.3 %collective-permute-start.6 = (bf16[1,64,2048]{2,1,0:T(8,128)(2,1)S(1)}, bf16[1,64,2048]{2,1,0:T(8,128)(2,1)S(1)}, u32[]{:S(2)}, u32[]{:S(2)}) collective-permute-start(bf16[1,64,2048]{2,1,0:T(8,128)(2,1)S(1)} %get-tuple-element.224), channel_id=1, source_target_pairs={{0,12},{4,0},{8,4},{12,8},{1,13},{5,1},{9,5},{13,9},{2,14},{6,2},{... | collective-permute-start | bytes 786440 | tf_op jit(solution)/shard_map/ppermute | solution.py:18
  89.7 23.3 %collective-permute-start.7 = (bf16[1,64,2048]{2,1,0:T(8,128)(2,1)S(1)}, bf16[1,64,2048]{2,1,0:T(8,128)(2,1)S(1)}, u32[]{:S(2)}, u32[]{:S(2)}) collective-permute-start(bf16[1,64,2048]{2,1,0:T(8,128)(2,1)S(1)} %get-tuple-element.223), channel_id=1, source_target_pairs={{0,8},{4,12},{8,0},{12,4},{1,9},{5,13},{9,1},{13,5},{2,10},{6,14},... | collective-permute-start | bytes 786440 | tf_op jit(solution)/shard_map/ppermute | solution.py:18
  89.7 23.3 %collective-permute-start.8 = (bf16[1,64,2048]{2,1,0:T(8,128)(2,1)S(1)}, bf16[1,64,2048]{2,1,0:T(8,128)(2,1)S(1)}, u32[]{:S(2)}, u32[]{:S(2)}) collective-permute-start(bf16[1,64,2048]{2,1,0:T(8,128)(2,1)S(1)} %get-tuple-element.222), channel_id=1, source_target_pairs={{0,4},{4,8},{8,12},{12,0},{1,5},{5,9},{9,13},{13,1},{2,6},{6,10},{... | collective-permute-start | bytes 786440 | tf_op jit(solution)/shard_map/ppermute | solution.py:18
  113.1 0.9 copy-start.1
  114.0 11.3 %collective-permute-start = (bf16[1,64,1024]{2,1,0:T(8,128)(2,1)S(1)}, bf16[1,64,1024]{2,1,0:T(8,128)(2,1)S(1)}, u32[]{:S(2)}, u32[]{:S(2)}) collective-permute-start(bf16[1,64,1024]{2,1,0:T(8,128)(2,1)S(1)} %copy.23), channel_id=1, source_target_pairs={{0,4},{4,8},{8,12},{12,0},{1,5},{5,9},{9,13},{13,1},{2,6},{6,10},{... | collective-permute-start | bytes 393224 | tf_op jit(solution)/shard_map/while/body/eval_jaxpr/ppermute | solution.py:43
  118.2 9.8 %collective-permute-start.1 = (f32[1,64,1024]{2,1,0:T(8,128)S(1)}, f32[1,64,1024]{2,1,0:T(8,128)S(1)}, u32[]{:S(2)}, u32[]{:S(2)}) collective-permute-start(f32[1,64,1024]{2,1,0:T(8,128)S(1)} %fusion.46), channel_id=1, source_target_pairs={{0,4},{4,8},{8,12},{12,0},{1,5},{5,9},{9,13},{13,1},{2,6},{6,10},{... | collective-permute-start | bytes 786440 | tf_op jit(solution)/shard_map/while/body/eval_jaxpr/ppermute | solution.py:43
  128.0 12.0 %collective-permute-start = (bf16[1,64,1024]{2,1,0:T(8,128)(2,1)S(1)}, bf16[1,64,1024]{2,1,0:T(8,128)(2,1)S(1)}, u32[]{:S(2)}, u32[]{:S(2)}) collective-permute-start(bf16[1,64,1024]{2,1,0:T(8,128)(2,1)S(1)} %copy.23), channel_id=1, source_target_pairs={{0,4},{4,8},{8,12},{12,0},{1,5},{5,9},{9,13},{13,1},{2,6},{6,10},{... | collective-permute-start | bytes 393224 | tf_op jit(solution)/shard_map/while/body/eval_jaxpr/ppermute | solution.py:43
  131.8 8.7 %collective-permute-start.1 = (f32[1,64,1024]{2,1,0:T(8,128)S(1)}, f32[1,64,1024]{2,1,0:T(8,128)S(1)}, u32[]{:S(2)}, u32[]{:S(2)}) collective-permute-start(f32[1,64,1024]{2,1,0:T(8,128)S(1)} %fusion.46), channel_id=1, source_target_pairs={{0,4},{4,8},{8,12},{12,0},{1,5},{5,9},{9,13},{13,1},{2,6},{6,10},{... | collective-permute-start | bytes 786440 | tf_op jit(solution)/shard_map/while/body/eval_jaxpr/ppermute | solution.py:43
  140.5 14.6 %collective-permute-start = (bf16[1,64,1024]{2,1,0:T(8,128)(2,1)S(1)}, bf16[1,64,1024]{2,1,0:T(8,128)(2,1)S(1)}, u32[]{:S(2)}, u32[]{:S(2)}) collective-permute-start(bf16[1,64,1024]{2,1,0:T(8,128)(2,1)S(1)} %copy.23), channel_id=1, source_target_pairs={{0,4},{4,8},{8,12},{12,0},{1,5},{5,9},{9,13},{13,1},{2,6},{6,10},{... | collective-permute-start | bytes 393224 | tf_op jit(solution)/shard_map/while/body/eval_jaxpr/ppermute | solution.py:43
  144.3 10.8 %collective-permute-start.1 = (f32[1,64,1024]{2,1,0:T(8,128)S(1)}, f32[1,64,1024]{2,1,0:T(8,128)S(1)}, u32[]{:S(2)}, u32[]{:S(2)}) collective-permute-start(f32[1,64,1024]{2,1,0:T(8,128)S(1)} %fusion.46), channel_id=1, source_target_pairs={{0,4},{4,8},{8,12},{12,0},{1,5},{5,9},{9,13},{13,1},{2,6},{6,10},{... | collective-permute-start | bytes 786440 | tf_op jit(solution)/shard_map/while/body/eval_jaxpr/ppermute | solution.py:43
  155.1 12.4 %collective-permute-start = (bf16[1,64,1024]{2,1,0:T(8,128)(2,1)S(1)}, bf16[1,64,1024]{2,1,0:T(8,128)(2,1)S(1)}, u32[]{:S(2)}, u32[]{:S(2)}) collective-permute-start(bf16[1,64,1024]{2,1,0:T(8,128)(2,1)S(1)} %copy.23), channel_id=1, source_target_pairs={{0,4},{4,8},{8,12},{12,0},{1,5},{5,9},{9,13},{13,1},{2,6},{6,10},{... | collective-permute-start | bytes 393224 | tf_op jit(solution)/shard_map/while/body/eval_jaxpr/ppermute | solution.py:43
  158.9 8.7 %collective-permute-start.1 = (f32[1,64,1024]{2,1,0:T(8,128)S(1)}, f32[1,64,1024]{2,1,0:T(8,128)S(1)}, u32[]{:S(2)}, u32[]{:S(2)}) collective-permute-start(f32[1,64,1024]{2,1,0:T(8,128)S(1)} %fusion.46), channel_id=1, source_target_pairs={{0,4},{4,8},{8,12},{12,0},{1,5},{5,9},{9,13},{13,1},{2,6},{6,10},{... | collective-permute-start | bytes 786440 | tf_op jit(solution)/shard_map/while/body/eval_jaxpr/ppermute | solution.py:43
Sparse Core Ops, SparseCore 0:
  167.7 71.5 reduce-scatter.1
